TPU v7x, 512 devices: a whole 4x8x8 slice. The times are simulated.
512 devices in a mesh: gx: 32 (over z_hi, y, core), gz: 16 (over z_lo, x).
Axes of the slice: x: 4, y: 8, z: 8 (z_hi: 2, z_lo: 4; z = z_hi * 4 + z_lo), core: 2. Of those that a mesh axis runs over, the one named last changes fastest.
Arguments:
- velocity: float32 [3, 2, 6144, 4096], P(None, None, 'gz', 'gx'), may hold values from -6 to 6
- metric_index: int32 [4096], P('gx'), may hold values from 0 to 63
- jac_table: float32 [64], replicated, may hold values from 0.5 to 2
- bend_table: float32 [64], replicated, may hold values from -1 to 1
Outputs:
- first_derivative: float32 [3, 2, 6144, 4096], P(None, None, 'gz', 'gx')
- second_derivative: float32 [3, 2, 6144, 4096], P(None, None, 'gz', 'gx')
- plane_energy: float32 [3, 2], replicated
Inputs may be any that keep to these rules, and one draw needn't show every extreme that they name: `metric_index`: each entry names a row of the metric tables.
All inputs are finite; a program needn't handle non-finite values.
Results may differ from a plain program's by a relative error of at most 0.00007.
Values sent between devices are 32-bit elements; how exact they have to be, the bound alone decides.
A program may use at most 64 MiB of HBM per device.

v0:
```python
import math
import jax
import jax.numpy as jnp
from jax import lax
from jax.sharding import PartitionSpec as P

alpha_one = 1.0 / 3.0
alpha_two = 2.0 / 11.0
reach = 24
highest = lax.Precision.HIGHEST


def band_matrix(rows, alpha):
    root = math.sqrt(1.0 - 4.0 * alpha * alpha)
    ratio = (1.0 - root) / (2.0 * alpha)
    factor = ratio / alpha / (1.0 - ratio * ratio)
    row_ids = jnp.arange(rows, dtype=jnp.int32)[:, None]
    col_ids = jnp.arange(rows + 2 * reach, dtype=jnp.int32)[None, :]
    offset = jnp.abs(col_ids - reach - row_ids)
    parity = jnp.where(offset % 2 == 0, 1.0, -1.0)
    power = jnp.exp(offset.astype(jnp.float32) * math.log(ratio))
    return jnp.where(offset <= reach, factor * parity * power, 0.0)


def stencil_matrix(rows, weights):
    row_ids = jnp.arange(rows, dtype=jnp.int32)[:, None]
    col_ids = jnp.arange(rows + 4, dtype=jnp.int32)[None, :]
    shift_ids = col_ids - row_ids - 2
    total = jnp.zeros((rows, rows + 4), jnp.float32)
    for shift_k, weight in zip((-2, -1, 0, 1, 2), weights):
        total = total + jnp.where(shift_ids == shift_k, weight, 0.0)
    return total


def line_operator(alpha, weights):
    block = 128
    band = band_matrix(block, alpha)
    stencil = stencil_matrix(block + 2 * reach, weights)
    joined = jnp.dot(band, stencil, precision=highest)
    start = block - reach - 2
    return jnp.pad(joined, ((0, 0), (start, 3 * block - start - joined.shape[1])))


def periodic_lines(columns):
    block = 128
    length = columns.shape[-1]
    lead = columns.shape[:-1]
    main = columns.reshape(lead + (length // block, block))
    before = jnp.roll(main, 1, axis=-2)
    after = jnp.roll(main, -1, axis=-2)
    weights_one = (-1.0 / 36.0, -7.0 / 9.0, 0.0, 7.0 / 9.0, 1.0 / 36.0)
    weights_two = (3.0 / 44.0, 12.0 / 11.0, -102.0 / 44.0, 12.0 / 11.0, 3.0 / 44.0)
    results = []
    for alpha, weights in ((alpha_one, weights_one), (alpha_two, weights_two)):
        whole_op = line_operator(alpha, weights)
        part = jnp.einsum("abcnm,im->abcni", before, whole_op[:, :block], precision=highest)
        part = part + jnp.einsum(
            "abcnm,im->abcni", main, whole_op[:, block : 2 * block], precision=highest
        )
        part = part + jnp.einsum(
            "abcnm,im->abcni", after, whole_op[:, 2 * block :], precision=highest
        )
        results.append(part.reshape(lead + (length,)))
    return (results[0], results[1])


def on_device(velocity, metric_index, jac_table, bend_table):
    first_line, second_line = periodic_lines(
        lax.all_to_all(velocity, "gx", split_axis=2, concat_axis=3, tiled=True)
    )
    first_xi = lax.all_to_all(first_line, "gx", split_axis=3, concat_axis=2, tiled=True)
    second_xi = lax.all_to_all(second_line, "gx", split_axis=3, concat_axis=2, tiled=True)
    table_rows = jac_table.shape[0]
    onehot = (metric_index[:, None] == jnp.arange(table_rows, dtype=jnp.int32)[None, :]).astype(
        jnp.float32
    )
    jac = jnp.dot(onehot, jac_table, precision=highest)
    bend = jnp.dot(onehot, bend_table, precision=highest)
    first = first_xi / jac
    second = (second_xi - bend * first) / (jac * jac)
    total_points = (
        metric_index.shape[0] * lax.axis_size("gx") * velocity.shape[2] * lax.axis_size("gz")
    )
    sums = lax.psum(jnp.sum(first * first, axis=(2, 3)), ("gx", "gz"))
    return (first, second, sums / total_points)


def solution(mesh):
    in_specs = (P(None, None, "gz", "gx"), P("gx"), P(), P())
    out_specs = (P(None, None, "gz", "gx"), P(None, None, "gz", "gx"), P())
    return jax.shard_map(
        on_device, mesh=mesh, in_specs=in_specs, out_specs=out_specs, check_vma=False
    )
```

profile of v0, /device:TPU:1, one launch (start us, length us, event | category | flops | bytes accessed | tf_op | source)
XLA Modules:
  0.0 331.4 jit_solution(7821478155496641981)
XLA Ops:
  0.6 3.2 copy.49
  3.9 17.2 %all-to-all-start = ((f32[3,2,384,128]{3,0,1,2:T(4,128)}), f32[3,2,384,128]{3,0,1,2:T(4,128)S(1)}, u32[]{:S(2)}, u32[]{:S(2)}) async-start(f32[3,2,384,128]{3,0,1,2:T(4,128)} %copy.49), calls=%async_computation | async-start | bytes 3145728 | tf_op jit(solution)/shard_map/all_to_all | solution.py:69
  21.1 1.1 fusion.18
  22.2 41.3 %all-to-all-done = f32[3,2,384,128]{3,0,1,2:T(4,128)S(1)} async-done(((f32[3,2,384,128]{3,0,1,2:T(4,128)}), f32[3,2,384,128]{3,0,1,2:T(4,128)S(1)}, u32[]{:S(2)}, u32[]{:S(2)}) %all-to-all-start) | async-done | bytes 1179680 | tf_op jit(solution)/shard_map/all_to_all | solution.py:69
  63.5 0.7 copy.92
  65.2 1.1 fusion.7
  66.4 1.1 fusion.5
  67.4 2.2 fusion.1
  69.6 11.0 %copy.89 = f32[3,2,12,32,128]{2,1,0,4,3:T(2,128)} copy(f32[3,2,12,32,128]{4,3,2,1,0:T(8,128)} %fusion.1) | data formatting | bytes 2359296 | tf_op jit(solution)/shard_map/reshape | solution.py:63
  80.6 19.5 %reshape.37 = f32[32,1,9216]{2,1,0:T(1,128)} reshape(f32[4096,3,2,12]{3,2,1,0:T(2,128)} %bitcast.61) | data formatting | bytes 2359296
  100.1 6.5 %all-to-all-start.1 = ((f32[32,1,9216]{2,1,0:T(1,128)}), f32[32,1,9216]{2,1,0:T(1,128)}, u32[]{:S(2)}, u32[]{:S(2)}) async-start(f32[32,1,9216]{2,1,0:T(1,128)} %reshape.37), calls=%async_computation.1 | async-start | bytes 2359296 | tf_op jit(solution)/shard_map/all_to_all | solution.py:71
  107.4 1.1 fusion.6
  108.5 1.1 fusion.4
  109.6 1.1 fusion.3
  110.7 9.0 %copy.90 = f32[3,2,12,32,128]{2,1,0,4,3:T(2,128)} copy(f32[3,2,12,32,128]{4,3,2,1,0:T(8,128)S(1)} %fusion.3) | data formatting | bytes 2359296 | tf_op jit(solution)/shard_map/reshape | solution.py:63
  119.8 19.5 %reshape.39 = f32[32,1,9216]{2,1,0:T(1,128)} reshape(f32[4096,3,2,12]{3,2,1,0:T(2,128)} %bitcast.62) | data formatting | bytes 2359296
  139.3 0.7 all-to-all-done.1
  140.0 11.7 %all-to-all-start.2 = ((f32[32,1,9216]{2,1,0:T(1,128)}), f32[32,1,9216]{2,1,0:T(1,128)S(1)}, u32[]{:S(2)}, u32[]{:S(2)}) async-start(f32[32,1,9216]{2,1,0:T(1,128)} %reshape.39), calls=%async_computation.2 | async-start | bytes 2359296 | tf_op jit(solution)/shard_map/all_to_all | solution.py:72
  151.9 0.6 broadcast.111
  152.4 4.8 %reduce.2 = f32[32,9216]{1,0:T(8,128)S(1)} reduce(f32[32,1,9216]{2,1,0:T(1,128)} %all-to-all-done.1, f32[]{:T(128)} %broadcast.111), dimensions={1}, to_apply=%all_to_all.40.reduce_sub_computation | reduce | bytes 2359300 | tf_op jit(solution)/shard_map/all_to_all | solution.py:71
  157.2 21.8 %reshape.38 = f32[4096,3,2,12]{3,2,1,0:T(2,128)} reshape(f32[32,9216]{1,0:T(8,128)S(1)} %reduce.2) | data formatting | bytes 2359296
  179.1 10.2 %copy.82 = f32[3,2,12,32,128]{4,3,1,2,0:T(8,128)S(1)} copy(f32[3,2,12,32,128]{2,1,0,4,3:T(2,128)} %bitcast.63) | data formatting | bytes 2359296 | tf_op jit(solution)/shard_map/all_to_all | solution.py:71
  190.1 100.3 %psum.7 = f32[3,2]{1,0:T(4,128)S(1)} all-reduce(f32[3,2]{1,0:T(4,128)S(1)} %multiply_reduce_fusion), channel_id=1, replica_groups=mesh['gx'=32,'gz'=16] {'gx','gz'}, use_global_device_ids=true, to_apply=%region_1.2 | all-reduce | flops 6 | bytes 48 | tf_op jit(solution)/shard_map/psum | solution.py:84
  290.4 0.7 copy.68
  291.0 0.9 copy.58
  291.9 3.5 %reduce.1 = f32[32,9216]{1,0:T(8,128)S(1)} reduce(f32[32,1,9216]{2,1,0:T(1,128)S(1)} %all-to-all-done.2, f32[]{:T(128)} %broadcast.111), dimensions={1}, to_apply=%all_to_all.44.reduce_sub_computation | reduce | bytes 2359300 | tf_op jit(solution)/shard_map/all_to_all | solution.py:72
  295.5 21.8 %reshape.40 = f32[4096,3,2,12]{3,2,1,0:T(2,128)} reshape(f32[32,9216]{1,0:T(8,128)S(1)} %reduce.1) | data formatting | bytes 2359296
  317.3 10.2 %copy.88 = f32[3,2,12,32,128]{4,3,1,2,0:T(8,128)S(1)} copy(f32[3,2,12,32,128]{2,1,0,4,3:T(2,128)} %bitcast.64) | data formatting | bytes 2359296 | tf_op jit(solution)/shard_map/all_to_all | solution.py:72
  327.5 0.9 copy.65
  328.4 0.8 subtract_divide_fusion
  329.2 1.1 copy.67
  330.3 1.1 copy.66
  (27 shorter events, 2.8 us)
Async XLA Ops:
  0.6 151.0 %copy-start = (f32[64]{0:T(128)S(1)}, f32[64]{0:T(128)}, u32[]{:S(2)}) copy-start(f32[64]{0:T(128)} %param.6) | copy-start | bytes 772
  3.9 59.7 %all-to-all-start = ((f32[3,2,384,128]{3,0,1,2:T(4,128)}), f32[3,2,384,128]{3,0,1,2:T(4,128)S(1)}, u32[]{:S(2)}, u32[]{:S(2)}) async-start(f32[3,2,384,128]{3,0,1,2:T(4,128)} %copy.49), calls=%async_computation | async-start | bytes 3145728 | tf_op jit(solution)/shard_map/all_to_all | solution.py:69
  64.3 0.6 copy-start.5
  64.3 2.0 copy-start.3
  64.3 0.9 copy-start.2
  100.1 39.8 %all-to-all-start.1 = ((f32[32,1,9216]{2,1,0:T(1,128)}), f32[32,1,9216]{2,1,0:T(1,128)}, u32[]{:S(2)}, u32[]{:S(2)}) async-start(f32[32,1,9216]{2,1,0:T(1,128)} %reshape.37), calls=%async_computation.1 | async-start | bytes 2359296 | tf_op jit(solution)/shard_map/all_to_all | solution.py:71
  106.6 0.8 copy-start.6
  107.4 1.1 copy-start.4
  139.3 12.4 %copy-start.7 = (s32[128]{0:T(128)S(1)}, s32[128]{0:T(128)}, u32[]{:S(2)}) copy-start(s32[128]{0:T(128)} %param.5) | copy-start | bytes 1540
  140.0 152.0 %all-to-all-start.2 = ((f32[32,1,9216]{2,1,0:T(1,128)}), f32[32,1,9216]{2,1,0:T(1,128)S(1)}, u32[]{:S(2)}, u32[]{:S(2)}) async-start(f32[32,1,9216]{2,1,0:T(1,128)} %reshape.39), calls=%async_computation.2 | async-start | bytes 2359296 | tf_op jit(solution)/shard_map/all_to_all | solution.py:72
  189.2 0.7 copy-start.8
  330.3 1.1 copy-start.1
where the time goes:
time: 333 us; the launch traced here: 331 us
  local copies, waits for them, and re-layouts  134 us (40%)
  blocking collectives  100 us (30%)
  waiting for transfers between devices  42 us (13%)
  starting transfers between devices  35.3 us (11%)
  matrix products  9.68 us (3%)
  other arithmetic  9.4 us (3%)
    psum x1, blocking collectives, on_device(): sums = lax.psum(jnp.sum(first * first, axis=(2, 3)), ('gx', 'gz'))  100 us
    unnamed x26, local copies, waits for them, and re-layouts  90.1 us
    all_to_all x1, waiting for transfers between devices, on_device(): lax.all_to_all(velocity, 'gx', split_axis=2, concat_axis=3, tiled=True)  41.3 us
    reshape x2, local copies, waits for them, and re-layouts, periodic_lines(): results.append(part.reshape(lead + (length,)))  20 us
    all_to_all x1, starting transfers between devices, on_device(): lax.all_to_all(velocity, 'gx', split_axis=2, concat_axis=3, tiled=True)  17.2 us
    all_to_all x1, starting transfers between devices, on_device(): lax.all_to_all(second_line, 'gx', split_axis=3, concat_axis=2, tiled=True)  11.7 us
    all_to_all x3, local copies, waits for them, and re-layouts, on_device(): lax.all_to_all(second_line, 'gx', split_axis=3, concat_axis=2, tiled=True)  11.6 us
    all_to_all x2, local copies, waits for them, and re-layouts, on_device(): lax.all_to_all(first_line, 'gx', split_axis=3, concat_axis=2, tiled=True)  11.1 us
  transfers between devices with their start and end apart: 3, of which 2 were waited for; matrix products, arithmetic and copies ran while one was open for 22% of the time, Pallas kernels for 0%

commit v1 on v0

--- a/solution.py
+++ b/solution.py
@@ -81,7 +81,7 @@
     total_points = (
         metric_index.shape[0] * lax.axis_size("gx") * velocity.shape[2] * lax.axis_size("gz")
     )
-    sums = lax.psum(jnp.sum(first * first, axis=(2, 3)), ("gx", "gz"))
+    sums = jnp.sum(lax.all_gather(jnp.sum(first * first, axis=(2, 3)), ("gx", "gz")), axis=0)
     return (first, second, sums / total_points)
 
 

time: 333 us -> 1560 us (4.68)
  the two profiles are of different devices: /device:TPU:1 before, /device:TPU:32 now
where the time goes in v1:
time: 1560 us; the launch traced here: 1550 us
  blocking collectives  1320 us (85%)
  local copies, waits for them, and re-layouts  133 us (9%)
  waiting for transfers between devices  38.9 us (2%)
  starting transfers between devices  38 us (2%)
    all_gather x1, blocking collectives, on_device(): lax.all_gather(jnp.sum(first * first, axis=(2, 3)), ('gx', 'gz'))  1320 us
    unnamed x27, local copies, waits for them, and re-layouts  89 us
    all_to_all x1, waiting for transfers between devices, on_device(): lax.all_to_all(velocity, 'gx', split_axis=2, concat_axis=3, tiled=True)  38.9 us
  transfers between devices with their start and end apart: 3, of which 1 were waited for; matrix products, arithmetic and copies ran while one was open for 5% of the time, Pallas kernels for 0%

profile of v1, /device:TPU:32, one launch (start us, length us, event | category | flops | bytes accessed | tf_op | source)
XLA Modules:
  0.0 1551.0 jit_solution(6842137458442270101)
XLA Ops:
  0.6 3.2 copy.49
  3.9 15.8 %all-to-all-start = ((f32[3,2,384,128]{3,0,1,2:T(4,128)}), f32[3,2,384,128]{3,0,1,2:T(4,128)S(1)}, u32[]{:S(2)}, u32[]{:S(2)}) async-start(f32[3,2,384,128]{3,0,1,2:T(4,128)} %copy.49), calls=%async_computation | async-start | bytes 3145728 | tf_op jit(solution)/shard_map/all_to_all | solution.py:69
  19.7 1.1 fusion.18
  20.8 38.9 %all-to-all-done = f32[3,2,384,128]{3,0,1,2:T(4,128)S(1)} async-done(((f32[3,2,384,128]{3,0,1,2:T(4,128)}), f32[3,2,384,128]{3,0,1,2:T(4,128)S(1)}, u32[]{:S(2)}, u32[]{:S(2)}) %all-to-all-start) | async-done | bytes 1179680 | tf_op jit(solution)/shard_map/all_to_all | solution.py:69
  59.8 0.7 copy.92
  61.5 1.1 fusion.7
  62.6 1.1 fusion.5
  63.7 2.2 fusion.1
  65.9 10.8 copy.89
  76.7 19.5 %reshape.41 = f32[32,1,9216]{2,1,0:T(1,128)} reshape(f32[4096,3,2,12]{3,2,1,0:T(2,128)} %bitcast.62) | data formatting | bytes 2359296
  96.2 9.3 all-to-all-start.1
  106.2 1.1 fusion.6
  107.3 1.1 fusion.4
  108.4 1.1 fusion.3
  109.6 9.0 copy.90
  118.6 19.5 %reshape.43 = f32[32,1,9216]{2,1,0:T(1,128)} reshape(f32[4096,3,2,12]{3,2,1,0:T(2,128)} %bitcast.63) | data formatting | bytes 2359296
  138.1 12.9 all-to-all-start.2
  151.3 0.8 fusion.142
  152.6 4.8 reduce.3
  157.4 21.8 %reshape.42 = f32[4096,3,2,12]{3,2,1,0:T(2,128)} reshape(f32[32,9216]{1,0:T(8,128)S(1)} %reduce.3) | data formatting | bytes 2359296
  179.2 10.2 copy.82
  189.7 0.9 copy.58
  190.7 1319.5 %all-gather.1 = f32[512,3,2]{1,2,0:T(2,128)S(1)} all-gather(f32[1,3,2]{1,2,0:T(2,128)S(1)} %bitcast.75), channel_id=2, replica_groups=mesh['gx'=32,'gz'=16] {'gx','gz'}, dimensions={0}, use_global_device_ids=true | all-gather | bytes 12312 | tf_op jit(solution)/shard_map/all_gather | solution.py:84
  1510.2 0.6 reduce_sum.19
  1510.7 0.6 broadcast_multiply_fusion
  1511.3 3.5 reduce.2
  1514.8 21.8 %reshape.44 = f32[4096,3,2,12]{3,2,1,0:T(2,128)} reshape(f32[32,9216]{1,0:T(8,128)S(1)} %reduce.2) | data formatting | bytes 2359296
  1536.7 10.2 copy.88
  1546.8 0.9 copy.65
  1547.8 0.8 subtract_divide_fusion
  1548.6 1.1 copy.68
  1549.7 1.1 copy.67
  (30 shorter events, 2.8 us)
Async XLA Ops:
  0.6 150.7 %copy-start = (f32[64]{0:T(128)S(1)}, f32[64]{0:T(128)}, u32[]{:S(2)}) copy-start(f32[64]{0:T(128)} %param.6) | copy-start | bytes 772
  3.9 55.9 %all-to-all-start = ((f32[3,2,384,128]{3,0,1,2:T(4,128)}), f32[3,2,384,128]{3,0,1,2:T(4,128)S(1)}, u32[]{:S(2)}, u32[]{:S(2)}) async-start(f32[3,2,384,128]{3,0,1,2:T(4,128)} %copy.49), calls=%async_computation | async-start | bytes 3145728 | tf_op jit(solution)/shard_map/all_to_all | solution.py:69
  60.5 0.6 copy-start.5
  60.5 2.0 copy-start.3
  60.5 0.9 copy-start.2
  96.2 42.0 %all-to-all-start.1 = ((f32[32,1,9216]{2,1,0:T(1,128)}), f32[32,1,9216]{2,1,0:T(1,128)}, u32[]{:S(2)}, u32[]{:S(2)}) async-start(f32[32,1,9216]{2,1,0:T(1,128)} %reshape.41), calls=%async_computation.1 | async-start | bytes 2359296 | tf_op jit(solution)/shard_map/all_to_all | solution.py:71
  105.5 0.8 copy-start.6
  106.2 1.1 copy-start.4
  138.1 13.0 copy-start.8
  138.1 13.0 copy-start.9
  138.1 1373.2 %all-to-all-start.2 = ((f32[32,1,9216]{2,1,0:T(1,128)}), f32[32,1,9216]{2,1,0:T(1,128)S(1)}, u32[]{:S(2)}, u32[]{:S(2)}) async-start(f32[32,1,9216]{2,1,0:T(1,128)} %reshape.43), calls=%async_computation.2 | async-start | bytes 2359296 | tf_op jit(solution)/shard_map/all_to_all | solution.py:72
  1546.8 0.9 copy-start.7
  1549.7 1.1 copy-start.1
